TPU v7x, 32 devices: a whole 2x2x4 slice. The times are simulated.
32 devices in a mesh: row: 4 (over y, x), col: 8 (over z, core).
Axes of the slice: x: 2, y: 2, z: 4, core: 2. Of those that a mesh axis runs over, the one named last changes fastest.
Arguments:
- parent_front: bfloat16 [28672, 28672], P('row', 'col'), may hold values from -6 to 6
- child_update: bfloat16 [2, 14336, 14336], P(None, 'row', 'col'), may hold values from -6 to 6
- parent_test: bfloat16 [28672, 448], P('col'), may hold values from -0.03125 to 0.03125
- child_test: bfloat16 [2, 14336, 448], P(None, 'col'), may hold values from -0.046875 to 0.046875
- child_map: int32 [2, 112], replicated, may hold values from 0 to 223, as said below
Outputs:
- leaf_basis: bfloat16 [224, 128, 448], P('row', 'col')
- couplings: float32 [32, 448, 448], P('row', 'col')
Inputs may be any that keep to these rules, and one draw needn't show every extreme that they name: `child_map`: for each child the entries rise strictly along its blocks, and entry j is at least j.
All inputs are finite; a program needn't handle non-finite values.
Results may differ from a plain program's by a relative error of at most 0.006.
Values may be sent and summed in bfloat16 or wider, within the bound.
A program may use at most 192 MiB of HBM per device.

v0:
```python
import math
import jax
import jax.numpy as jnp
from jax import lax
from jax.sharding import PartitionSpec as P

LEAF = 896
BLOCK = 128
HIGH = lax.Precision.HIGHEST


def spread(block, axis, holder):
    block = jnp.where(lax.axis_index(axis) == holder, block, jnp.zeros_like(block))
    return lax.psum(block, axis)


def finish(leaves, gram_matrix):
    factor = jnp.linalg.cholesky(gram_matrix)
    solved = lax.linalg.triangular_solve(
        factor, leaves, left_side=False, lower=True, transpose_a=True
    )
    return (solved * math.sqrt(LEAF)).astype(jnp.bfloat16)


def local(parent_front, child_update, parent_test, child_test, child_map):
    row_count = lax.axis_size("row")
    col_count = lax.axis_size("col")
    row_index = lax.axis_index("row")
    col_index = lax.axis_index("col")
    slab_rows = BLOCK // col_count
    own_blocks = parent_front.shape[0] // BLOCK
    kid_blocks = child_update.shape[1] // BLOCK
    probes = parent_test.shape[1]
    own_probe = jnp.dot(parent_front, parent_test, preferred_element_type=jnp.float32)
    own_probe = own_probe.reshape(own_blocks, BLOCK, probes)
    kid_probe = jnp.stack(
        [
            jnp.dot(child_update[which], child_test[which], preferred_element_type=jnp.float32)
            for which in range(2)
        ]
    )
    kid_probe = kid_probe.reshape(2, kid_blocks, BLOCK, probes)
    own_share, kid_share = (
        lax.psum_scatter(own_probe, "col", scatter_dimension=1, tiled=True),
        lax.psum_scatter(kid_probe, "col", scatter_dimension=2, tiled=True),
    )
    first_block = row_index * own_blocks
    targets = jnp.arange(own_blocks, dtype=jnp.int32)
    mapped = child_map - first_block
    onehot = (mapped[:, None, :] == targets[None, :, None]).astype(jnp.float32)
    sample = own_share + jnp.einsum(
        "cpn,cnsr->psr",
        onehot,
        lax.all_gather(kid_share, "row", axis=1, tiled=True),
        precision=HIGH,
    )
    per_leaf = LEAF // BLOCK
    leaf_count = own_blocks // per_leaf
    leaves = sample.reshape(leaf_count, per_leaf * slab_rows, probes)
    partial_gram = jnp.einsum("lkr,lks->lrs", leaves, leaves, precision=HIGH)
    gram_matrix = lax.psum(partial_gram, "col")
    leaf_basis = finish(leaves, gram_matrix).reshape(own_blocks, slab_rows, probes)
    whole_basis = lax.all_gather(leaf_basis, "col", axis=1, tiled=True)
    bases = whole_basis.reshape(leaf_count, LEAF, probes)
    col_leaves = parent_front.shape[1] // LEAF
    shrink = 1.0 / math.sqrt(LEAF)

    def sibling_product(position):
        leaf_index = col_index * col_leaves + position
        sibling = jnp.bitwise_xor(leaf_index, 1)
        row_start = leaf_index % leaf_count * LEAF
        col_start = (sibling - col_index * col_leaves) * LEAF
        front_tile = lax.dynamic_slice(parent_front, (row_start, col_start), (LEAF, LEAF))
        product = (
            jnp.dot(front_tile, bases[sibling % leaf_count], preferred_element_type=jnp.float32)
            * shrink
        )
        return product.astype(jnp.bfloat16)

    products = lax.map(sibling_product, jnp.arange(col_leaves, dtype=jnp.int32))
    owner_span = col_count // row_count
    core_rows = probes // col_count
    received = [
        spread(products, "col", row_index * owner_span + offset) for offset in range(owner_span)
    ]
    products_all = jnp.concatenate(received, axis=0)
    columns = lax.dynamic_slice_in_dim(bases, col_index * core_rows, core_rows, 2)
    couplings = (
        jnp.einsum("lkr,lks->lrs", columns, products_all, preferred_element_type=jnp.float32)
        * shrink
    )
    return (leaf_basis, couplings)


def solution(mesh):
    in_specs = (P("row", "col"), P(None, "row", "col"), P("col", None), P(None, "col", None), P())
    out_specs = (P("row", "col", None), P("row", "col", None))
    return jax.shard_map(local, mesh=mesh, in_specs=in_specs, out_specs=out_specs, check_vma=False)
```

profile of v0, /device:TPU:0, one launch (start us, length us, event | category | flops | bytes accessed | tf_op | source)
XLA Modules:
  0.0 1988.0 jit_solution(7997422557833170795)
XLA Ops:
  7.2 9.5 fusion.77
  16.7 10.6 convolution_bitcast_fusion.1
  27.3 10.6 convolution_bitcast_fusion.2
  37.8 10.9 pad_maximum_fusion
  48.7 21.7 %copy.91 = f32[2,28,128,448]{3,0,1,2:T(2,128)} copy(f32[2,28,128,448]{2,3,1,0:T(8,128)} %pad_maximum_fusion) | data formatting | bytes 25690112 | tf_op jit(solution)/shard_map/stack | solution.py:36
  72.3 295.1 %all-reduce.11.cloned.1.call-done = f32[2,28,128,448]{3,0,1,2:T(2,128)} async-done(((f32[2,28,128,448]{3,0,1,2:T(2,128)}), f32[2,28,128,448]{3,0,1,2:T(2,128)}) %all-reduce.11.cloned.1.call-update) | async-done | bytes 12845072
  372.4 30.3 %convolution_bitcast_fusion = f32[56,8,56,128]{3,1,2,0:T(8,128)} fusion(bf16[7168,3584]{1,0:T(8,128)(2,1)} %param.7, bf16[3584,448]{0,1:T(8,128)(2,1)S(1)} %copy-done), kind=kOutput, calls=%fused_computation.11 | convolution fusion | flops 23018340352 | bytes 67436544 | tf_op jit(solution)/shard_map/dot_general | solution.py:34
  402.7 12.1 copy.136
  414.8 16.4 copy.90
  431.9 19.0 all-gather.3.cloned.1.call-done
  450.9 151.3 %reduce-scatter.2.cloned.1.call-done = f32[56,16,448]{2,0,1:T(8,128)} async-done(((f32[56,128,448]{2,0,1:T(8,128)}), f32[56,16,448]{2,0,1:T(8,128)}) %reduce-scatter.2.cloned.1.call-update) | async-done | bytes 1605648 | tf_op jit(solution)/shard_map/reduce_scatter | solution.py:44
  602.2 10.3 bitcast_add_fusion.1
  613.6 8.1 fusion.78
  623.1 153.0 %all-reduce.9.cloned.1.call-done = f32[8,448,448]{1,2,0:T(8,128)} async-done(((f32[8,448,448]{1,2,0:T(8,128)}), f32[8,448,448]{1,2,0:T(8,128)}) %all-reduce.9.cloned.1.call-update) | async-done | bytes 6422544 | tf_op jit(solution)/shard_map/psum | solution.py:61
  776.1 8.5 copy.97
  784.6 7.0 fusion.13
  791.6 2.9 copy-done.3
  794.6 93.8 %custom-call.34 = f32[8,128,128]{2,1,0:T(8,128)S(1)} custom-call(f32[8,128,128]{2,1,0:T(8,128)S(1)} %cholesky.281), custom_call_target="Cholesky" | custom-call | tf_op jit(solution)/shard_map/jit(cholesky)/cholesky | solution.py:18
  888.4 4.0 cholesky.236
  892.4 79.2 %custom-call.35 = f32[8,1,128,128]{2,3,1,0:T(8,128)} custom-call(f32[8,1,128,128]{3,2,1,0:T(8,128)S(1)} %select_bitcast_fusion.2), custom_call_target="InvertDiagBlocksLowerTriangular" | custom-call | tf_op jit(solution)/shard_map/jit(cholesky)/cholesky | solution.py:18
  971.7 3.9 constant_dynamic-update-slice_fusion.3
  975.5 2.7 convolution_subtract_fusion
  979.3 94.2 %custom-call.36 = f32[8,128,128]{2,1,0:T(8,128)S(1)} custom-call(f32[8,128,128]{2,1,0:T(8,128)S(1)} %cholesky.285), custom_call_target="Cholesky" | custom-call | tf_op jit(solution)/shard_map/jit(cholesky)/cholesky | solution.py:18
  1074.5 79.2 %custom-call.37 = f32[8,1,128,128]{2,3,1,0:T(8,128)} custom-call(f32[8,1,128,128]{3,2,1,0:T(8,128)S(1)} %get-tuple-element.154), custom_call_target="InvertDiagBlocksLowerTriangular" | custom-call | tf_op jit(solution)/shard_map/jit(cholesky)/cholesky | solution.py:18
  1153.8 3.1 convolution_dynamic-update-slice_fusion
  1156.9 3.6 fusion.38
  1161.3 95.4 %custom-call.38 = f32[8,128,128]{2,1,0:T(8,128)} custom-call(f32[8,128,128]{2,1,0:T(8,128)} %cholesky.290), custom_call_target="Cholesky" | custom-call | tf_op jit(solution)/shard_map/jit(cholesky)/cholesky | solution.py:18
  1259.1 79.4 %custom-call.39 = f32[8,1,128,128]{2,3,1,0:T(8,128)S(1)} custom-call(f32[8,1,128,128]{3,2,1,0:T(8,128)} %get-tuple-element.152), custom_call_target="InvertDiagBlocksLowerTriangular" | custom-call | tf_op jit(solution)/shard_map/jit(cholesky)/cholesky | solution.py:18
  1339.8 2.5 convolution_subtract_fusion.3
  1342.4 46.9 %custom-call.40 = f32[8,64,64]{2,1,0:T(8,128)S(1)} custom-call(f32[8,64,64]{2,1,0:T(8,128)S(1)} %convolution_subtract_fusion.3), custom_call_target="Cholesky" | custom-call | tf_op jit(solution)/shard_map/jit(cholesky)/cholesky | solution.py:18
  1390.4 4.3 select_select_fusion
  1394.8 2.9 copy-done.2
  1397.7 12.5 while.16
  1398.3 3.6 bitcast_dynamic-update-slice_fusion.3
  1402.4 3.6 bitcast_dynamic-update-slice_fusion.3
  1406.6 3.6 bitcast_dynamic-update-slice_fusion.3
  1410.5 3.0 pad_maximum_fusion.1
  1413.5 316.0 %custom-call.41 = f32[8,4,128,128]{2,3,1,0:T(8,128)} custom-call(f32[8,4,128,128]{3,2,1,0:T(8,128)} %pad_maximum_fusion.1), custom_call_target="InvertDiagBlocksLowerTriangular" | custom-call | tf_op jit(solution)/shard_map/triangular_solve | solution.py:19
  1737.2 3.1 fusion.41
  1742.5 73.5 %all-gather.5.cloned.1.call-done = bf16[56,128,448]{2,1,0:T(8,128)(2,1)} async-done(((bf16[56,16,448]{2,1,0:T(8,128)(2,1)}), bf16[56,128,448]{2,1,0:T(8,128)(2,1)}) %all-gather.5.cloned.1.call-update) | async-done | bytes 6422544 | tf_op jit(solution)/shard_map/all_gather | solution.py:63
  1816.0 17.0 while.15
  1817.6 2.8 fusion.100
  1821.7 2.8 fusion.100
  1825.9 2.9 fusion.100
  1830.2 2.8 fusion.100
  1833.0 3.2 broadcast_select_fusion.1
  1836.2 137.2 %all-reduce.13.cloned.1.call-done = (bf16[4,896,448]{1,2,0:T(8,128)(2,1)}, bf16[4,896,448]{1,2,0:T(8,128)(2,1)}) async-done(((bf16[4,896,448]{1,2,0:T(8,128)(2,1)}, bf16[4,896,448]{1,2,0:T(8,128)(2,1)}), (bf16[4,896,448]{1,2,0:T(8,128)(2,1)}, bf16[4,896,448]{1,2,0:T(8,128)(2,1)})) %all-reduce.13.cloned.1.call-update) | async-done | bytes 6422544 | tf_op jit(solution)/shard_map/psum | solution.py:14
  1973.5 7.4 fusion.52
  (82 shorter events, 31.6 us)
Async XLA Ops:
  7.2 365.2 %copy-start = (bf16[3584,448]{0,1:T(8,128)(2,1)S(1)}, bf16[3584,448]{0,1:T(8,128)(2,1)}, u32[]{:S(2)}) copy-start(bf16[3584,448]{0,1:T(8,128)(2,1)} %param.9) | copy-start | bytes 9633796
  7.2 360.2 %all-reduce.11.cloned.1.call-start = ((), (), s32[]{:S(2)}) async-start(), calls=%async_computation.5 | async-start | bytes 29360128
  70.4 0.7 copy-start.10
  70.4 380.5 %all-gather.3.cloned.1.call-start = ((), (), s32[]{:S(2)}) async-start(), calls=%async_computation.2 | async-start | bytes 9175040 | tf_op jit(solution)/shard_map/all_gather | solution.py:54
  371.8 230.4 %reduce-scatter.2.cloned.1.call-start = ((), (), s32[]{:S(2)}) async-start(), calls=%async_computation.1 | async-start | bytes 16515072 | tf_op jit(solution)/shard_map/reduce_scatter | solution.py:44
  431.2 0.7 copy-start.9
  431.2 344.9 %all-reduce.9.cloned.1.call-start = ((), (), s32[]{:S(2)}) async-start(), calls=%async_computation.3 | async-start | bytes 14680064 | tf_op jit(solution)/shard_map/psum | solution.py:61
  621.7 1194.3 %all-gather.5.cloned.1.call-start = ((), (), s32[]{:S(2)}) async-start(), calls=%async_computation.4 | async-start | bytes 8257536 | tf_op jit(solution)/shard_map/all_gather | solution.py:63
  791.6 2.9 copy-start.3
  888.4 4.0 copy-start.5
  978.2 1.1 copy-start.4
  1073.5 80.2 %copy-start.7 = (f32[8,128,128]{2,1,0:T(8,128)}, f32[8,128,128]{2,1,0:T(8,128)S(1)}, u32[]{:S(2)}) copy-start(f32[8,128,128]{2,1,0:T(8,128)S(1)} %custom-call.36) | copy-start | bytes 1572868
  1153.8 102.9 %copy-start.6 = (f32[8,128,128]{2,1,0:T(8,128)S(1)}, f32[8,128,128]{2,1,0:T(8,128)}, u32[]{:S(2)}) copy-start(f32[8,128,128]{2,1,0:T(8,128)} %copy-done.5) | copy-start | bytes 1572868
  1394.7 2.9 copy-start.2
  1729.5 4.1 copy-start.8
  1742.4 231.1 %all-reduce.13.cloned.1.call-start = ((), (), s32[]{:S(2)}) async-start(), calls=%async_computation.6 | async-start | bytes 12845056 | tf_op jit(solution)/shard_map/psum | solution.py:14
  1973.5 7.4 copy-start.1
Sparse Core Ops, SparseCore 0:
  70.5 296.7 all-reduce.10
  371.9 78.9 all-gather.2
  453.2 148.9 reduce-scatter.1
  621.9 154.2 all-reduce.8
  1742.5 73.4 all-gather.4
  1836.3 137.0 all-reduce.12
where the time goes:
time: 2000 us; the launch traced here: 1990 us
  other arithmetic  919 us (46%)
  waiting for transfers between devices  829 us (41%)
  matrix products  118 us (6%)
  local copies, waits for them, and re-layouts  102 us (5%)
    another operation x18, other arithmetic, finish(): factor = jnp.linalg.cholesky(gram_matrix)  573 us
    another operation x8, other arithmetic, finish(): lax.linalg.triangular_solve(factor, leaves, left_side=False, lower=True,...  324 us
    unnamed x7, waiting for transfers between devices  295 us
    psum x1, waiting for transfers between devices, local(): gram_matrix = lax.psum(partial_gram, 'col')  153 us
    reduce_scatter x1, waiting for transfers between devices, local(): lax.psum_scatter(own_probe, 'col', scatter_dimension=1, tiled=True)  151 us
    psum x1, waiting for transfers between devices, spread(): return lax.psum(block, axis)  137 us
    all_gather x1, waiting for transfers between devices, local(): whole_basis = lax.all_gather(leaf_basis, 'col', axis=1, tiled=True)  73.5 us
  transfers between devices with their start and end apart: 6, of which 6 were waited for; matrix products, arithmetic and copies ran while one was open for 3% of the time, Pallas kernels for 0%

commit v1 on v0

--- a/solution.py
+++ b/solution.py
@@ -58,7 +58,7 @@
     leaf_count = own_blocks // per_leaf
     leaves = sample.reshape(leaf_count, per_leaf * slab_rows, probes)
     partial_gram = jnp.einsum("lkr,lks->lrs", leaves, leaves, precision=HIGH)
-    gram_matrix = lax.psum(partial_gram, "col")
+    gram_matrix = jnp.sum(lax.all_gather(partial_gram, "col"), axis=0)
     leaf_basis = finish(leaves, gram_matrix).reshape(own_blocks, slab_rows, probes)
     whole_basis = lax.all_gather(leaf_basis, "col", axis=1, tiled=True)
     bases = whole_basis.reshape(leaf_count, LEAF, probes)

time: 2000 us -> 2360 us (1.18)
  waiting for transfers between devices: 829 us -> 1170 us
    all_gather x0 -> x1, waiting for transfers between devices: none -> 493 us  [local(): gram_matrix = jnp.sum(lax.all_gather(partial_gram, 'col'), axis=0)]
    psum x1 -> x0, waiting for transfers between devices: 153 us -> none  [local(): gram_matrix = lax.psum(partial_gram, 'col')]
where the time goes in v1:
time: 2360 us; the launch traced here: 2350 us
  waiting for transfers between devices  1170 us (50%)
  other arithmetic  941 us (40%)
  matrix products  117 us (5%)
  local copies, waits for them, and re-layouts  102 us (4%)
    another operation x18, other arithmetic, finish(): factor = jnp.linalg.cholesky(gram_matrix)  572 us
    all_gather x1, waiting for transfers between devices, local(): gram_matrix = jnp.sum(lax.all_gather(partial_gram, 'col'), axis=0)  493 us
    another operation x8, other arithmetic, finish(): lax.linalg.triangular_solve(factor, leaves, left_side=False, lower=True,...  324 us
    unnamed x7, waiting for transfers between devices  295 us
    reduce_scatter x1, waiting for transfers between devices, local(): lax.psum_scatter(own_probe, 'col', scatter_dimension=1, tiled=True)  151 us
    psum x1, waiting for transfers between devices, spread(): return lax.psum(block, axis)  137 us
    all_gather x1, waiting for transfers between devices, local(): whole_basis = lax.all_gather(leaf_basis, 'col', axis=1, tiled=True)  71.6 us
  transfers between devices with their start and end apart: 6, of which 6 were waited for; matrix products, arithmetic and copies ran while one was open for 3% of the time, Pallas kernels for 0%

profile of v1, /device:TPU:0, one launch (start us, length us, event | category | flops | bytes accessed | tf_op | source)
XLA Modules:
  0.0 2347.9 jit_solution(12527099344854173640)
XLA Ops:
  7.2 9.5 fusion.77
  16.7 10.6 convolution_bitcast_fusion.1
  27.3 10.6 convolution_bitcast_fusion.2
  37.8 10.9 pad_maximum_fusion
  48.7 21.7 copy.87
  72.3 295.1 %all-reduce.8.cloned.1.call-done = f32[2,28,128,448]{3,0,1,2:T(2,128)} async-done(((f32[2,28,128,448]{3,0,1,2:T(2,128)}), f32[2,28,128,448]{3,0,1,2:T(2,128)}) %all-reduce.8.cloned.1.call-update) | async-done | bytes 12845072
  372.1 30.3 %convolution_bitcast_fusion = f32[56,8,56,128]{3,1,2,0:T(8,128)} fusion(bf16[7168,3584]{1,0:T(8,128)(2,1)} %param.7, bf16[3584,448]{0,1:T(8,128)(2,1)S(1)} %copy-done), kind=kOutput, calls=%fused_computation.11 | convolution fusion | flops 23018340352 | bytes 67436544 | tf_op jit(solution)/shard_map/dot_general | solution.py:34
  402.4 12.2 copy.131
  414.6 16.4 copy.86
  431.7 19.2 all-gather.5.cloned.1.call-done
  450.9 151.3 %reduce-scatter.2.cloned.1.call-done = f32[56,16,448]{2,0,1:T(8,128)} async-done(((f32[56,128,448]{2,0,1:T(8,128)}), f32[56,16,448]{2,0,1:T(8,128)}) %reduce-scatter.2.cloned.1.call-update) | async-done | bytes 1605648 | tf_op jit(solution)/shard_map/reduce_scatter | solution.py:44
  602.2 10.3 bitcast_add_fusion.1
  613.7 8.0 fusion.78
  623.3 492.5 %all-gather.9.cloned.1.call-done = f32[64,448,448]{2,1,0:T(8,128)} async-done(((f32[8,448,448]{2,1,0:T(8,128)}), f32[64,448,448]{2,1,0:T(8,128)}) %all-gather.9.cloned.1.call-update) | async-done | bytes 51380240 | tf_op jit(solution)/shard_map/all_gather | solution.py:61
  1115.8 22.0 reduce_sum.9
  1137.9 8.5 copy.92
  1146.4 7.0 fusion.13
  1153.4 2.9 copy-done.3
  1156.4 93.8 %custom-call.34 = f32[8,128,128]{2,1,0:T(8,128)S(1)} custom-call(f32[8,128,128]{2,1,0:T(8,128)S(1)} %cholesky.281), custom_call_target="Cholesky" | custom-call | tf_op jit(solution)/shard_map/jit(cholesky)/cholesky | solution.py:18
  1250.2 4.0 cholesky.236
  1254.2 79.4 %custom-call.35 = f32[8,1,128,128]{2,3,1,0:T(8,128)} custom-call(f32[8,1,128,128]{3,2,1,0:T(8,128)S(1)} %select_bitcast_fusion.2), custom_call_target="InvertDiagBlocksLowerTriangular" | custom-call | tf_op jit(solution)/shard_map/jit(cholesky)/cholesky | solution.py:18
  1333.6 3.9 constant_dynamic-update-slice_fusion.3
  1337.5 2.7 convolution_subtract_fusion
  1341.3 93.8 %custom-call.36 = f32[8,128,128]{2,1,0:T(8,128)S(1)} custom-call(f32[8,128,128]{2,1,0:T(8,128)S(1)} %cholesky.285), custom_call_target="Cholesky" | custom-call | tf_op jit(solution)/shard_map/jit(cholesky)/cholesky | solution.py:18
  1436.1 79.2 %custom-call.37 = f32[8,1,128,128]{2,3,1,0:T(8,128)} custom-call(f32[8,1,128,128]{3,2,1,0:T(8,128)S(1)} %get-tuple-element.154), custom_call_target="InvertDiagBlocksLowerTriangular" | custom-call | tf_op jit(solution)/shard_map/jit(cholesky)/cholesky | solution.py:18
  1515.3 3.1 convolution_dynamic-update-slice_fusion
  1518.4 3.6 fusion.38
  1522.8 95.4 %custom-call.38 = f32[8,128,128]{2,1,0:T(8,128)} custom-call(f32[8,128,128]{2,1,0:T(8,128)} %cholesky.290), custom_call_target="Cholesky" | custom-call | tf_op jit(solution)/shard_map/jit(cholesky)/cholesky | solution.py:18
  1620.6 79.4 %custom-call.39 = f32[8,1,128,128]{2,3,1,0:T(8,128)S(1)} custom-call(f32[8,1,128,128]{3,2,1,0:T(8,128)} %get-tuple-element.152), custom_call_target="InvertDiagBlocksLowerTriangular" | custom-call | tf_op jit(solution)/shard_map/jit(cholesky)/cholesky | solution.py:18
  1703.9 46.9 %custom-call.40 = f32[8,64,64]{2,1,0:T(8,128)S(1)} custom-call(f32[8,64,64]{2,1,0:T(8,128)S(1)} %convolution_subtract_fusion.3), custom_call_target="Cholesky" | custom-call | tf_op jit(solution)/shard_map/jit(cholesky)/cholesky | solution.py:18
  1752.0 4.3 select_select_fusion
  1756.4 2.9 copy-done.2
  1759.3 12.5 while.16
  1759.9 3.6 bitcast_dynamic-update-slice_fusion.3
  1764.0 3.6 bitcast_dynamic-update-slice_fusion.3
  1768.2 3.6 bitcast_dynamic-update-slice_fusion.3
  1772.0 3.0 pad_maximum_fusion.1
  1775.0 316.1 %custom-call.41 = f32[8,4,128,128]{2,3,1,0:T(8,128)} custom-call(f32[8,4,128,128]{3,2,1,0:T(8,128)} %pad_maximum_fusion.1), custom_call_target="InvertDiagBlocksLowerTriangular" | custom-call | tf_op jit(solution)/shard_map/triangular_solve | solution.py:19
  2098.8 3.1 fusion.41
  2104.1 71.6 %all-gather.7.cloned.1.call-done = bf16[56,128,448]{2,1,0:T(8,128)(2,1)} async-done(((bf16[56,16,448]{2,1,0:T(8,128)(2,1)}), bf16[56,128,448]{2,1,0:T(8,128)(2,1)}) %all-gather.7.cloned.1.call-update) | async-done | bytes 6422544 | tf_op jit(solution)/shard_map/all_gather | solution.py:63
  2175.7 17.0 while.15
  2177.3 2.8 fusion.100
  2181.5 2.8 fusion.100
  2185.7 2.8 fusion.100
  2189.8 2.8 fusion.100
  2192.7 3.2 broadcast_select_fusion.1
  2195.9 137.2 %all-reduce.10.cloned.1.call-done = (bf16[4,896,448]{1,2,0:T(8,128)(2,1)}, bf16[4,896,448]{1,2,0:T(8,128)(2,1)}) async-done(((bf16[4,896,448]{1,2,0:T(8,128)(2,1)}, bf16[4,896,448]{1,2,0:T(8,128)(2,1)}), (bf16[4,896,448]{1,2,0:T(8,128)(2,1)}, bf16[4,896,448]{1,2,0:T(8,128)(2,1)})) %all-reduce.10.cloned.1.call-update) | async-done | bytes 6422544 | tf_op jit(solution)/shard_map/psum | solution.py:14
  2333.1 7.4 fusion.52
  (83 shorter events, 34.1 us)
Async XLA Ops:
  7.2 364.9 %copy-start = (bf16[3584,448]{0,1:T(8,128)(2,1)S(1)}, bf16[3584,448]{0,1:T(8,128)(2,1)}, u32[]{:S(2)}) copy-start(bf16[3584,448]{0,1:T(8,128)(2,1)} %param.9) | copy-start | bytes 9633796
  7.2 360.2 %all-reduce.8.cloned.1.call-start = ((), (), s32[]{:S(2)}) async-start(), calls=%async_computation.5 | async-start | bytes 29360128
  70.4 0.7 copy-start.10
  70.4 380.5 %all-gather.5.cloned.1.call-start = ((), (), s32[]{:S(2)}) async-start(), calls=%async_computation.2 | async-start | bytes 9175040 | tf_op jit(solution)/shard_map/all_gather | solution.py:54
  371.8 230.4 %reduce-scatter.2.cloned.1.call-start = ((), (), s32[]{:S(2)}) async-start(), calls=%async_computation.1 | async-start | bytes 16515072 | tf_op jit(solution)/shard_map/reduce_scatter | solution.py:44
  431.1 0.7 copy-start.9
  431.1 684.8 %all-gather.9.cloned.1.call-start = ((), (), s32[]{:S(2)}) async-start(), calls=%async_computation.4 | async-start | bytes 66060288 | tf_op jit(solution)/shard_map/all_gather | solution.py:61
  621.7 1554.0 %all-gather.7.cloned.1.call-start = ((), (), s32[]{:S(2)}) async-start(), calls=%async_computation.3 | async-start | bytes 8257536 | tf_op jit(solution)/shard_map/all_gather | solution.py:63
  1153.4 2.9 copy-start.3
  1250.2 4.0 copy-start.5
  1340.2 1.1 copy-start.4
  1435.1 80.2 %copy-start.7 = (f32[8,128,128]{2,1,0:T(8,128)}, f32[8,128,128]{2,1,0:T(8,128)S(1)}, u32[]{:S(2)}) copy-start(f32[8,128,128]{2,1,0:T(8,128)S(1)} %custom-call.36) | copy-start | bytes 1572868
  1515.3 103.0 %copy-start.6 = (f32[8,128,128]{2,1,0:T(8,128)S(1)}, f32[8,128,128]{2,1,0:T(8,128)}, u32[]{:S(2)}) copy-start(f32[8,128,128]{2,1,0:T(8,128)} %copy-done.5) | copy-start | bytes 1572868
  1756.3 2.9 copy-start.2
  2091.1 4.1 copy-start.8
  2104.0 229.1 %all-reduce.10.cloned.1.call-start = ((), (), s32[]{:S(2)}) async-start(), calls=%async_computation.6 | async-start | bytes 12845056 | tf_op jit(solution)/shard_map/psum | solution.py:14
  2333.1 7.4 copy-start.1
Sparse Core Ops, SparseCore 0:
  70.5 296.7 all-reduce.7
  371.9 78.9 all-gather.4
  453.3 148.9 reduce-scatter.1
  621.8 493.9 all-gather.8
  2104.1 71.5 all-gather.6
  2196.0 137.0 all-reduce.9
